TPU v7x, 32 devices: a whole 2x2x4 slice. The times are simulated.
32 devices in a mesh: groups: 2 (over x), out: 16 (over z, y, core).
Axes of the slice: x: 2, y: 2, z: 4, core: 2. Of those that a mesh axis runs over, the one named last changes fastest.
Arguments:
- stream: bfloat16 [128, 12288], P('groups', 'out'), parts along dimension 0, may hold values from -6 to 6
- norm_gain: float32 [12288], replicated, may hold values from 0.5 to 1.5
- w_query: bfloat16 [12288, 6144], P(None, 'out')
- w_keyval: bfloat16 [12288, 1024], P(None, 'out'), may hold values from -0.0546875 to 0.0546875
- w_out: bfloat16 [6144, 12288], P('out'), may hold values from -0.75 to 0.75
- lengths: int32 [128], P(('groups', 'out')), parts along dimension 0, may hold values from 1 to 512, as said below
- key_cache: bfloat16 [128, 512, 512], P(('groups', 'out')), parts along dimension 0, may hold values from -127 to 127, as said below
- value_cache: bfloat16 [128, 512, 512], P(('groups', 'out')), parts along dimension 0, may hold values from -127 to 127, as said below
- key_scales: int32 [128, 4, 4], P(('groups', 'out')), parts along dimension 0, may hold values from -8 to -6
- value_scales: int32 [128, 4, 4], P(('groups', 'out')), parts along dimension 0, may hold values from -8 to -6
Outputs:
- new_stream: bfloat16 [128, 12288], P('groups', 'out'), parts along dimension 0
There are 2 independent parts, one for each index of `groups`. A program takes and returns all parts, laid end to end along the dimension named above; an argument that names none is the same for every part. Nothing has to cross between parts.
Inputs may be any that keep to these rules, and one draw needn't show every extreme that they name: `lengths`: every row holds at least one earlier token; in every draw some row holds exactly 512. `key_cache`: whole numbers, codes of an eight-bit cache. `value_cache`: whole numbers, codes of an eight-bit cache.
All inputs are finite; a program needn't handle non-finite values.
Results may differ from a plain program's by a relative error of at most 0.024.
The roundings to bfloat16 on the way count: a program that leaves them out, or rounds other values in their place, can miss the bound.
Values may be sent and summed in bfloat16 or wider, within the bound.
No kernel may reach another device: no remote copies, remote signals or barrier semaphores. Data moves between devices by JAX's collectives and lax.ppermute only.
A program may use at most 64 MiB of HBM per device.

v0:
```python
import math

import jax
import jax.numpy as jnp
from jax import lax
from jax.experimental import pallas as pl
from jax.experimental.pallas import tpu as pltpu
from jax.sharding import PartitionSpec as P


HQ = 48
KVH = 4
HD = 128


rope_base = 1000000.0
norm_eps = 1e-05


def rotate(vec, position):
    half = vec.shape[-1] // 2
    index = jnp.arange(half, dtype=jnp.float32)
    freq = jnp.exp(index * (-2.0 * math.log(rope_base) / vec.shape[-1]))
    angle = position * freq
    cosine = jnp.cos(angle)
    sine = jnp.sin(angle)
    first = vec[..., :half]
    second = vec[..., half:]
    return jnp.concatenate(
        [first * cosine - second * sine, second * cosine + first * sine], axis=-1
    )


def dequant(cache, scales):
    rows, span, width = cache.shape
    blocks = scales.shape[1]
    factor = jnp.exp2(scales.astype(jnp.float32)).astype(jnp.bfloat16)
    shaped = cache.reshape(rows, blocks, span // blocks, KVH, width // KVH)
    return (shaped * factor[:, :, None, :, None]).reshape(rows, span, KVH, width // KVH)


def per_device_general(
    stream,
    norm_gain,
    w_query,
    w_keyval,
    w_out,
    lengths,
    key_cache,
    value_cache,
    key_scales,
    value_scales,
):
    local_rows = lengths.shape[0]
    xf = stream.astype(jnp.float32)
    whole = lax.all_gather(stream, "out", axis=1, tiled=True).astype(jnp.float32)
    meansq = jnp.mean(whole * whole, axis=-1, keepdims=True)
    normed = (whole * lax.rsqrt(meansq + norm_eps) * norm_gain).astype(jnp.bfloat16)
    q_local = jnp.dot(normed, w_query, preferred_element_type=jnp.float32).astype(jnp.bfloat16)
    kv_local = jnp.dot(normed, w_keyval, preferred_element_type=jnp.float32).astype(jnp.bfloat16)
    q_rows, kv_rows = (
        lax.all_to_all(q_local, "out", split_axis=0, concat_axis=1, tiled=True),
        lax.all_to_all(kv_local, "out", split_axis=0, concat_axis=1, tiled=True),
    )
    position = lengths.astype(jnp.float32)[:, None, None]
    rotated = rotate(q_rows.astype(jnp.float32).reshape(local_rows, HQ, HD), position).astype(
        jnp.bfloat16
    )
    rotated = rotated.reshape(local_rows, KVH, HQ // KVH, HD)
    new_key = rotate(
        kv_rows[:, : KVH * HD].astype(jnp.float32).reshape(local_rows, KVH, HD), position
    ).astype(jnp.bfloat16)
    new_value = kv_rows[:, KVH * HD :].reshape(local_rows, KVH, HD)
    factor = HD ** (-0.5)
    own = jnp.einsum("rkgd,rkd->rkg", rotated, new_key, preferred_element_type=jnp.float32) * factor
    span = key_cache.shape[1]
    scores = (
        jnp.einsum(
            "rkgd,rjkd->rkgj",
            rotated,
            dequant(key_cache, key_scales),
            preferred_element_type=jnp.float32,
        )
        * factor
    )
    valid = jnp.arange(span, dtype=jnp.int32)[None, :] < lengths[:, None]
    scores = jnp.where(valid[:, None, None, :], scores, -jnp.inf)
    top = jnp.maximum(jnp.max(scores, axis=-1), own)
    weights = jnp.exp(scores - top[..., None])
    own_weight = jnp.exp(own - top)
    total = jnp.sum(weights, axis=-1) + own_weight
    own_rounded = lax.optimization_barrier(own_weight.astype(jnp.bfloat16)).astype(jnp.float32)
    summed = jnp.einsum(
        "rkgj,rjkd->rkgd",
        weights.astype(jnp.bfloat16),
        dequant(value_cache, value_scales),
        preferred_element_type=jnp.float32,
    )
    summed = summed + own_rounded[..., None] * new_value.astype(jnp.float32)[:, :, None, :]
    attended = (summed / total[..., None]).astype(jnp.bfloat16).reshape(local_rows, HQ * HD)
    heads = lax.all_to_all(attended, "out", split_axis=1, concat_axis=0, tiled=True)
    partial_terms = jnp.dot(heads, w_out, preferred_element_type=jnp.float32)
    projected = lax.psum_scatter(partial_terms, "out", scatter_dimension=1, tiled=True)
    return (xf + projected).astype(jnp.bfloat16)


def swapped(value, mask, size):
    return lax.ppermute(value, "out", [(i, i ^ mask) for i in range(size)])


def room_kernel(out_ref):
    pass


def stage_kernel(*refs):
    refs[-1][...] = jnp.zeros_like(refs[-1])


def stage(cover):
    vmem = pl.BlockSpec(memory_space=pltpu.VMEM)
    small = pltpu.CompilerParams(vmem_limit_bytes=2 * 1024 * 1024)
    room = pl.pallas_call(
        room_kernel,
        out_shape=jax.ShapeDtypeStruct((2048, 512), jnp.bfloat16),
        out_specs=vmem,
        compiler_params=small,
        name="room",
    )()
    count = -(-cover // (2 * room.size))
    return pl.pallas_call(
        stage_kernel,
        out_shape=jax.ShapeDtypeStruct((8, 128), jnp.float32),
        in_specs=[pl.BlockSpec(memory_space=pl.ANY)] * count,
        out_specs=vmem,
        compiler_params=small,
        name="stage",
    )(*[room] * count)


def project_kernel(order, pieces, *refs):
    shards = refs[:pieces]
    gain_ref, wq_ref, wkv_ref, _, out_ref = refs[pieces:]
    rows, depth = shards[0].shape
    columns, kv_columns = wq_ref.shape[1], wkv_ref.shape[0]
    targets, per_target, _ = out_ref.shape
    me = lax.axis_index("out")
    square = jnp.zeros((rows, 128), jnp.float32)
    for k in range(pieces):
        part = shards[k][...].astype(jnp.float32)
        part = part * part
        for lane in range(0, depth, 128):
            square += part[:, lane : lane + 128]
    meansq = jnp.sum(square, axis=-1, keepdims=True) / (depth * pieces)
    inverse = lax.rsqrt(meansq + norm_eps)
    q_sum = jnp.zeros((rows, columns), jnp.float32)
    kv_sum = jnp.zeros((rows, kv_columns), jnp.float32)
    for k in range(pieces):
        start = pl.multiple_of(lax.bitwise_xor(me, order[k]) * depth, 128)
        gain = gain_ref[:, pl.ds(start, depth)]
        normed = (shards[k][...].astype(jnp.float32) * inverse * gain).astype(jnp.bfloat16)
        kv_sum += lax.dot_general(
            normed,
            wkv_ref[:, pl.ds(start, depth)],
            (((1,), (1,)), ((), ())),
            preferred_element_type=jnp.float32,
        )
        q_sum += jnp.dot(normed, wq_ref[pl.ds(start, depth), :], preferred_element_type=jnp.float32)
    odd = lax.bitwise_and(me, 1).astype(jnp.float32)
    both = jnp.concatenate([kv_sum * (1.0 - odd), kv_sum * odd], axis=-1)
    for k in range(targets):
        take = slice(k * per_target, (k + 1) * per_target)
        out_ref[k, :, :columns] = q_sum[take].astype(jnp.bfloat16)
        out_ref[k, :, columns:] = both[take].astype(jnp.bfloat16)


def project(order, shards, norm_gain, w_query, w_keyval, mark, per_target):
    pieces = len(shards)
    rows = shards[0].shape[0]
    vmem = pl.BlockSpec(memory_space=pltpu.VMEM)
    return pl.pallas_call(
        lambda *refs: project_kernel(order, pieces, *refs),
        out_shape=jax.ShapeDtypeStruct(
            (rows // per_target, per_target, w_query.shape[1] + 2 * w_keyval.shape[0]), jnp.bfloat16
        ),
        in_specs=[vmem] * (pieces + 4),
        out_specs=vmem,
        compiler_params=pltpu.CompilerParams(vmem_limit_bytes=16 * 1024 * 1024),
        name="project",
    )(*shards, norm_gain, w_query, w_keyval, mark)


def attend_kernel(
    lengths_ref, rows_ref, cos_ref, sin_ref, kf_ref, vf_ref, keys_ref, values_ref, out_ref
):
    sources, local_rows, _ = rows_ref.shape
    span = keys_ref.shape[1]
    each = out_ref.shape[-1] // HD
    heads = each * sources
    per_key = HQ // KVH // each
    blocks = kf_ref.shape[1]
    per_block = span // blocks
    each_row = range(local_rows)
    key_head = lax.broadcasted_iota(jnp.int32, (heads, HD), 0) % sources // per_key
    block_head = lax.broadcasted_iota(jnp.int32, (sources, per_block), 0) // per_key
    pick_row = lax.broadcasted_iota(jnp.int32, (2 * sources, sources), 0)
    pick_col = lax.broadcasted_iota(jnp.int32, (2 * sources, sources), 1)
    wanted = (pick_row % sources) // per_key + KVH * (pick_row // sources)
    pick = (pick_col // 2 == wanted).astype(jnp.bfloat16)
    place = lax.broadcasted_iota(jnp.int32, (heads, span), 1)

    def scaled(values, scale_ref, r):
        parts = []
        for b in range(blocks):
            scale = jnp.full((sources, per_block), scale_ref[r, b, 0])
            for k in range(1, KVH):
                scale = jnp.where(block_head == k, scale_ref[r, b, k], scale)
            scale = jnp.concatenate([scale] * each, axis=0)
            parts.append(values[:, b * per_block : (b + 1) * per_block] * scale)
        return jnp.concatenate(parts, axis=1)

    def turn(vec, r):
        cosine, sine = cos_ref[r : r + 1, :], sin_ref[r : r + 1, :]
        turned = vec * cosine + pltpu.roll(vec, HD // 2, 1) * sine
        return turned.astype(jnp.bfloat16).astype(jnp.float32)

    got = [rows_ref[:, r, :].astype(jnp.float32) for r in each_row]
    fresh = jnp.dot(
        pick,
        jnp.concatenate([g[:, each * HD :] for g in got], axis=1).astype(jnp.bfloat16),
        preferred_element_type=jnp.float32,
    )
    query, scores = [], []
    for r in each_row:
        query.append(
            turn(
                jnp.concatenate([got[r][:, g * HD : (g + 1) * HD] for g in range(each)], axis=0), r
            )
        )
        wide = jnp.concatenate(
            [jnp.where(key_head == k, query[r], 0.0) for k in range(KVH)], axis=1
        ).astype(jnp.bfloat16)
        scores.append(
            lax.dot_general(
                wide, keys_ref[r], (((1,), (1,)), ((), ())), preferred_element_type=jnp.float32
            )
        )
    own_weight, total, summed = [], [], []
    for r in each_row:
        new_key = turn(fresh[:sources, r * HD : (r + 1) * HD], r)
        new_key = jnp.concatenate([new_key] * each, axis=0)
        own = jnp.sum(query[r] * new_key, axis=-1, keepdims=True) * HD ** (-0.5)
        score = scaled(scores[r], kf_ref, r) * HD ** (-0.5)
        score = jnp.where(place < lengths_ref[r], score, -jnp.inf)
        top = jnp.maximum(jnp.max(score, axis=-1, keepdims=True), own)
        weights = jnp.exp(score - top)
        own_weight.append(jnp.exp(own - top))
        total.append(jnp.sum(weights, axis=-1, keepdims=True) + own_weight[r])
        rounded = scaled(weights.astype(jnp.bfloat16).astype(jnp.float32), vf_ref, r)
        summed.append(
            jnp.dot(
                rounded.astype(jnp.bfloat16), values_ref[r], preferred_element_type=jnp.float32
            )
        )
    for r in each_row:
        mine = summed[r][:, :HD]
        for k in range(1, KVH):
            mine = jnp.where(key_head == k, summed[r][:, k * HD : (k + 1) * HD], mine)
        new_value = jnp.concatenate([fresh[sources:, r * HD : (r + 1) * HD]] * each, axis=0)
        mine = mine + own_weight[r].astype(jnp.bfloat16).astype(jnp.float32) * new_value
        mine = (mine / total[r]).astype(jnp.bfloat16)
        for g in range(each):
            out_ref[:, r, g * HD : (g + 1) * HD] = mine[g * sources : (g + 1) * sources]


def attend(rows, columns, lengths, cosine, sine, key_factors, value_factors, key_cache, value_cache):
    sources, local_rows, _ = rows.shape
    smem = pl.BlockSpec(memory_space=pltpu.SMEM)
    vmem = pl.BlockSpec(memory_space=pltpu.VMEM)
    return pl.pallas_call(
        attend_kernel,
        out_shape=jax.ShapeDtypeStruct((sources, local_rows, columns), jnp.bfloat16),
        in_specs=[smem] + [vmem] * 3 + [smem] * 2 + [vmem] * 2,
        out_specs=vmem,
        compiler_params=pltpu.CompilerParams(vmem_limit_bytes=8 * 1024 * 1024),
        name="attend",
    )(lengths, rows, cosine, sine, key_factors, value_factors, key_cache, value_cache)


def expand_kernel(order, heads_ref, w_ref, out_ref):
    width = out_ref.shape[-1]
    me = lax.axis_index("out")
    heads = jnp.concatenate(
        [heads_ref[k].astype(jnp.float32) for k in range(heads_ref.shape[0])], axis=0
    ).astype(jnp.bfloat16)
    for k in range(len(order)):
        start = pl.multiple_of(lax.bitwise_xor(me, order[k]) * width, 128)
        out_ref[k] = jnp.dot(
            heads, w_ref[:, pl.ds(start, width)], preferred_element_type=jnp.float32
        ).astype(out_ref.dtype)


def expand(order, heads, w_out, width, dtype):
    vmem = pl.BlockSpec(memory_space=pltpu.VMEM)
    return pl.pallas_call(
        lambda *refs: expand_kernel(order, *refs),
        out_shape=jax.ShapeDtypeStruct(
            (len(order), heads.shape[0] * heads.shape[1], width), dtype
        ),
        in_specs=[vmem, vmem],
        out_specs=vmem,
        compiler_params=pltpu.CompilerParams(vmem_limit_bytes=16 * 1024 * 1024),
        name="expand",
    )(heads, w_out)


def per_device(
    size,
    stream,
    norm_gain,
    w_query,
    w_keyval,
    w_out,
    lengths,
    key_cache,
    value_cache,
    key_scales,
    value_scales,
):
    local_rows = lengths.shape[0]
    width = stream.shape[1]
    columns = w_query.shape[1]

    block = [m for m in (2, 4, 6) if m < size]
    tops = [1 << k for k in range(3, size.bit_length() - 1)]
    w_keyval = w_keyval.T
    norm_gain = norm_gain.reshape(1, -1)
    held = {0: stream}
    for bit in tops[::-1]:
        for mask in list(held):
            held[mask | bit] = swapped(held[mask], bit, size)
    last = max(held)
    held[last], mark = lax.optimization_barrier(
        (held[last], stage(2 * (w_query.size + w_keyval.size + w_out.size)))
    )
    for mask in list(held):
        for over in block:
            held[mask | over] = swapped(held[mask], over, size)
    for mask in list(held):
        held[mask | 1] = swapped(held[mask], 1, size)
    order = list(held)
    freq = jnp.exp(
        jnp.arange(HD // 2, dtype=jnp.float32) * (-2.0 * math.log(rope_base) / HD)
    )
    angle = lengths.astype(jnp.float32)[:, None] * freq
    cosine, sine = jnp.cos(angle), jnp.sin(angle)
    side = (
        jnp.concatenate([cosine, cosine], axis=-1),
        jnp.concatenate([-sine, sine], axis=-1),
        jnp.exp2(key_scales.astype(jnp.float32)),
        jnp.exp2(value_scales.astype(jnp.float32)),
    )
    side, held[size - 1] = lax.optimization_barrier((side, held[size - 1]))
    qkv = project(order, [held[m] for m in order], norm_gain, w_query, w_keyval, mark, local_rows)
    rows = lax.all_to_all(qkv, "out", split_axis=0, concat_axis=0, tiled=True)
    attended = attend(rows, columns, lengths, *side, key_cache, value_cache)
    heads = lax.all_to_all(attended, "out", split_axis=0, concat_axis=0, tiled=True)

    owed = {}
    spans = [t for t in range(0, size, 8)][::-1]
    for top in spans:
        near = [top | m for m in block + [0]]
        away = [m | 1 for m in near]
        sent = expand(away, heads, w_out, width, jnp.bfloat16)
        sent = swapped(sent, 1, size)
        kept = expand(near, heads, w_out, width, jnp.float32)
        for k, mask in enumerate(near):
            owed[mask] = kept[k] + sent[k].astype(jnp.float32)
        for mask in near[-2::-1]:
            got = swapped(owed[mask].astype(jnp.bfloat16), mask ^ top, size)
            owed[top] = owed[top] + got.astype(jnp.float32)
    for bit in tops[::-1]:
        for mask in [m for m in spans if m & bit and m < 2 * bit]:
            got = swapped(owed[mask].astype(jnp.bfloat16), bit, size)
            owed[mask ^ bit] = owed[mask ^ bit] + got.astype(jnp.float32)
    return (stream.astype(jnp.float32) + owed[0]).astype(jnp.bfloat16)


def solution(mesh):
    size = mesh.shape["out"]

    def step(stream, *rest):
        columns = rest[1].shape[1]
        whole_heads = columns % HD == 0 and HQ // KVH * HD % columns == 0 and 2 * rest[2].shape[1] == HD
        if size & (size - 1) == 0 and stream.shape[1] % 128 == 0 and whole_heads:
            return per_device(size, stream, *rest)
        return per_device_general(stream, *rest)

    return jax.shard_map(
        step,
        mesh=mesh,
        in_specs=(
            P("groups", "out"),
            P(),
            P(None, "out"),
            P(None, "out"),
            P("out", None),
            P(("groups", "out")),
            P(("groups", "out"), None, None),
            P(("groups", "out"), None, None),
            P(("groups", "out"), None, None),
            P(("groups", "out"), None, None),
        ),
        out_specs=P("groups", "out"),
        check_vma=False,
    )
```

profile of v0, /device:TPU:0, one launch (start us, length us, event | category | flops | bytes accessed | tf_op | source)
XLA Modules:
  0.0 64.4 jit_solution(3459935593893019610)
XLA Ops:
  0.0 4.1 %collective-permute-start = (bf16[64,768]{1,0:T(8,128)(2,1)}, bf16[64,768]{1,0:T(8,128)(2,1)S(1)}, u32[]{:S(2)}, u32[]{:S(2)}) collective-permute-start(bf16[64,768]{1,0:T(8,128)(2,1)} %refs_0_.1), channel_id=1, source_target_pairs={{0,8},{1,9},{2,10},{3,11},{4,12},{5,13},{6,14},{7,15},{8,0},{9,1},... | collective-permute-start | bytes 294920 | tf_op jit(solution)/shard_map/ppermute | solution.py:108
  4.1 1.5 %collective-permute-start.1 = (bf16[64,768]{1,0:T(8,128)(2,1)}, bf16[64,768]{1,0:T(8,128)(2,1)S(1)}, u32[]{:S(2)}, u32[]{:S(2)}) collective-permute-start(bf16[64,768]{1,0:T(8,128)(2,1)} %refs_0_.1), channel_id=1, source_target_pairs={{0,2},{1,3},{2,0},{3,1},{4,6},{5,7},{6,4},{7,5},{8,10},{9,11},{10,... | collective-permute-start | bytes 294920 | tf_op jit(solution)/shard_map/ppermute | solution.py:108
  5.6 1.6 %collective-permute-start.2 = (bf16[64,768]{1,0:T(8,128)(2,1)}, bf16[64,768]{1,0:T(8,128)(2,1)S(1)}, u32[]{:S(2)}, u32[]{:S(2)}) collective-permute-start(bf16[64,768]{1,0:T(8,128)(2,1)} %refs_0_.1), channel_id=1, source_target_pairs={{0,4},{1,5},{2,6},{3,7},{4,0},{5,1},{6,2},{7,3},{8,12},{9,13},{10,... | collective-permute-start | bytes 294920 | tf_op jit(solution)/shard_map/ppermute | solution.py:108
  7.2 0.4 collective-permute-start.3
  7.6 0.0 collective-permute-start.7
  7.6 0.7 %multiply_exponential_fusion = (f32[4,4,4]{2,1,0:T(4,128)S(1)}, f32[4,4,4]{2,1,0:T(4,128)S(1)}) fusion(s32[4,4,4]{2,1,0:T(4,128)} %param.19, s32[4,4,4]{2,1,0:T(4,128)} %param.18), kind=kLoop, calls=%fused_computation.32 | loop fusion | flops 256 | bytes 1024 | tf_op jit(solution)/shard_map/exp2 | solution.py:360
  8.3 0.0 copy-start.6
  8.3 0.0 copy-start
  8.3 0.0 copy-start.3
  8.3 0.0 copy-start.4
  8.4 0.0 copy-start.5
  8.4 0.0 slice-start
  8.4 0.0 slice-start.1
  8.4 0.6 copy-done.6
  9.0 0.3 collective-permute-done.refs_1_
  9.3 2.2 %collective-permute-start.6 = (bf16[64,768]{1,0:T(8,128)(2,1)S(1)}, bf16[64,768]{1,0:T(8,128)(2,1)S(1)}, u32[]{:S(2)}, u32[]{:S(2)}) collective-permute-start(bf16[64,768]{1,0:T(8,128)(2,1)S(1)} %collective-permute-done.refs_1_), channel_id=1, source_target_pairs={{0,6},{1,7},{2,4},{3,5},{4,2},{5,3},{6,0},{7,1},{8,14},{9,15},{10,... | collective-permute-start | bytes 294920 | tf_op jit(solution)/shard_map/ppermute | solution.py:108
  11.5 0.6 collective-permute-start.4
  12.1 0.0 collective-permute-done.2.refs_3_
  12.1 0.8 %collective-permute-start.5 = (bf16[64,768]{1,0:T(8,128)(2,1)S(1)}, bf16[64,768]{1,0:T(8,128)(2,1)S(1)}, u32[]{:S(2)}, u32[]{:S(2)}) collective-permute-start(bf16[64,768]{1,0:T(8,128)(2,1)S(1)} %collective-permute-done.refs_1_), channel_id=1, source_target_pairs={{0,4},{1,5},{2,6},{3,7},{4,0},{5,1},{6,2},{7,3},{8,12},{9,13},{10,... | collective-permute-start | bytes 294920 | tf_op jit(solution)/shard_map/ppermute | solution.py:108
  12.9 0.0 collective-permute-done.3.refs_4_
  12.9 2.3 %collective-permute-done.6.refs_7_ = bf16[64,768]{1,0:T(8,128)(2,1)S(1)} collective-permute-done((bf16[64,768]{1,0:T(8,128)(2,1)S(1)}, bf16[64,768]{1,0:T(8,128)(2,1)S(1)}, u32[]{:S(2)}, u32[]{:S(2)}) %collective-permute-start.6) | collective-permute-done | bytes 98336 | tf_op jit(solution)/shard_map/ppermute | solution.py:108
  15.2 0.1 fusion.24
  15.3 0.0 collective-permute-done.7.refs_8_
  15.3 0.6 collective-permute-start.9
  15.8 1.3 %collective-permute-done.4.refs_5_ = bf16[64,768]{1,0:T(8,128)(2,1)S(1)} collective-permute-done((bf16[64,768]{1,0:T(8,128)(2,1)S(1)}, bf16[64,768]{1,0:T(8,128)(2,1)S(1)}, u32[]{:S(2)}, u32[]{:S(2)}) %collective-permute-start.4) | collective-permute-done | bytes 98336 | tf_op jit(solution)/shard_map/ppermute | solution.py:108
  17.2 0.0 collective-permute-start.10
  17.2 0.0 collective-permute-done.5.refs_6_
  17.2 0.5 collective-permute-start.11
  17.7 0.1 collective-permute-start.12
  17.8 0.4 collective-permute-start.13
  18.2 0.1 pad_maximum_fusion
  18.3 0.2 collective-permute-done.10.refs_11_
  18.5 0.2 collective-permute-done.11.refs_12_
  18.6 0.4 collective-permute-done.12.refs_13_
  19.0 0.2 collective-permute-done.13.refs_14_
  19.2 0.0 copy-start.1
  19.2 0.0 copy-start.2
  19.2 0.0 slice-start.2
  19.2 2.5 %project.1 = bf16[16,4,512]{2,1,0:T(4,128)(2,1)S(1)} custom-call(bf16[64,768]{1,0:T(8,128)(2,1)S(1)} %copy-done.4, bf16[64,768]{1,0:T(8,128)(2,1)S(1)} %collective-permute-done.refs_1_, bf16[64,768]{1,0:T(8,128)(2,1)S(1)} %collective-permute-done.1.refs_2_, bf16[64,768]{1,0:T(8,128)(2,1)S(1)} %collective-permute-done.2.refs_3_, ...), custom_call_target="tpu_custom_call" | custom-call | tf_op jit(solution)/shard_map/project/pallas_call | solution.py:180
  21.7 11.9 %all_to_all.10.rows_ref = bf16[16,4,512]{2,1,0:T(4,128)(2,1)S(1)} all-to-all(bf16[16,4,512]{2,1,0:T(4,128)(2,1)S(1)} %project.1), channel_id=1, replica_groups=mesh['groups'=2,'out'=16] {'out'}, dimensions={0} | all-to-all | bytes 131072 | tf_op jit(solution)/shard_map/all_to_all | solution.py:364
  33.7 1.9 %attend.1 = bf16[16,4,384]{2,1,0:T(4,128)(2,1)S(1)} custom-call(s32[4]{0:T(128)S(1)} %copy-done.6, bf16[16,4,512]{2,1,0:T(4,128)(2,1)S(1)} %all_to_all.10.rows_ref, f32[4,128]{1,0:T(4,128)S(1)} %get-tuple-element.15.cos_ref, f32[4,128]{1,0:T(4,128)S(1)} %get-tuple-element.16.sin_ref, f32[4,4,4]{2,1,0:T(4,128)S(1)} %get-tuple-element.17.kf_ref, ...), custom_call_target="tpu_custom_call" | custom-call | tf_op jit(solution)/shard_map/attend/pallas_call | solution.py:279
  35.6 9.3 %all_to_all.11.refs_0_ = bf16[16,4,384]{2,1,0:T(4,128)(2,1)S(1)} all-to-all(bf16[16,4,384]{2,1,0:T(4,128)(2,1)S(1)} %attend.1), channel_id=1, replica_groups=mesh['groups'=2,'out'=16] {'out'}, dimensions={0} | all-to-all | bytes 98304 | tf_op jit(solution)/shard_map/all_to_all | solution.py:366
  45.0 0.6 expand.7
  45.6 0.1 collective-permute-start.19
  45.6 0.6 expand.5
  46.2 0.6 collective-permute-start.15
  46.8 0.6 expand.4
  47.4 0.6 expand.6
  48.0 0.1 fusion.21
  48.0 0.3 collective-permute-start.22
  48.3 0.6 collective-permute-start.21
  48.9 2.6 %collective-permute-start.20 = (bf16[64,768]{1,0:T(8,128)(2,1)S(1)}, bf16[64,768]{1,0:T(8,128)(2,1)S(1)}, u32[]{:S(2)}, u32[]{:S(2)}) collective-permute-start(bf16[64,768]{1,0:T(8,128)(2,1)S(1)} %get-tuple-element.22), channel_id=1, source_target_pairs={{0,6},{1,7},{2,4},{3,5},{4,2},{5,3},{6,0},{7,1},{8,14},{9,15},{10,... | collective-permute-start | bytes 294920 | tf_op jit(solution)/shard_map/ppermute | solution.py:108
  51.6 0.1 fusion.18
  51.6 0.3 collective-permute-start.18
  51.9 0.6 collective-permute-start.17
  52.6 0.2 collective-permute-done.22
  52.8 2.4 %collective-permute-start.16 = (bf16[64,768]{1,0:T(8,128)(2,1)S(1)}, bf16[64,768]{1,0:T(8,128)(2,1)S(1)}, u32[]{:S(2)}, u32[]{:S(2)}) collective-permute-start(bf16[64,768]{1,0:T(8,128)(2,1)S(1)} %get-tuple-element.19), channel_id=1, source_target_pairs={{0,6},{1,7},{2,4},{3,5},{4,2},{5,3},{6,0},{7,1},{8,14},{9,15},{10,... | collective-permute-start | bytes 294920 | tf_op jit(solution)/shard_map/ppermute | solution.py:108
  55.2 2.2 %collective-permute-done.20 = bf16[64,768]{1,0:T(8,128)(2,1)S(1)} collective-permute-done((bf16[64,768]{1,0:T(8,128)(2,1)S(1)}, bf16[64,768]{1,0:T(8,128)(2,1)S(1)}, u32[]{:S(2)}, u32[]{:S(2)}) %collective-permute-start.20) | collective-permute-done | bytes 98336 | tf_op jit(solution)/shard_map/ppermute | solution.py:108
  57.4 0.1 fusion.7
  57.5 0.4 collective-permute-start.23
  57.9 0.3 collective-permute-done.17
  58.1 3.2 %collective-permute-done.16 = bf16[64,768]{1,0:T(8,128)(2,1)S(1)} collective-permute-done((bf16[64,768]{1,0:T(8,128)(2,1)S(1)}, bf16[64,768]{1,0:T(8,128)(2,1)S(1)}, u32[]{:S(2)}, u32[]{:S(2)}) %collective-permute-start.16) | collective-permute-done | bytes 98336 | tf_op jit(solution)/shard_map/ppermute | solution.py:108
  61.4 2.3 %collective-permute-done.23 = bf16[64,768]{1,0:T(8,128)(2,1)S(1)} collective-permute-done((bf16[64,768]{1,0:T(8,128)(2,1)S(1)}, bf16[64,768]{1,0:T(8,128)(2,1)S(1)}, u32[]{:S(2)}, u32[]{:S(2)}) %collective-permute-start.23) | collective-permute-done | bytes 98336 | tf_op jit(solution)/shard_map/ppermute | solution.py:108
  63.6 0.7 %fusion.17 = bf16[64,768]{1,0:T(8,128)(2,1)} fusion(f32[4,64,768]{2,1,0:T(8,128)S(1)} %expand.4, bf16[64,768]{1,0:T(8,128)(2,1)S(1)} %collective-permute-done.23, bf16[64,768]{1,0:T(8,128)(2,1)S(1)} %collective-permute-done.18, bf16[64,768]{1,0:T(8,128)(2,1)S(1)} %collective-permute-done.17, bf16[64,768]{1,0:T(8,128)(2,1)S(1)} %collective-permute-done.16, ...), kind=kLoop, calls=%fused_computation.25 | loop fusion | flops 638976 | bytes 884736 | tf_op jit(solution)/shard_map/convert_element_type | solution.py:385
  (24 shorter events, 0.1 us)
Async XLA Ops:
  0.0 9.3 %collective-permute-start = (bf16[64,768]{1,0:T(8,128)(2,1)}, bf16[64,768]{1,0:T(8,128)(2,1)S(1)}, u32[]{:S(2)}, u32[]{:S(2)}) collective-permute-start(bf16[64,768]{1,0:T(8,128)(2,1)} %refs_0_.1), channel_id=1, source_target_pairs={{0,8},{1,9},{2,10},{3,11},{4,12},{5,13},{6,14},{7,15},{8,0},{9,1},... | collective-permute-start | bytes 294920 | tf_op jit(solution)/shard_map/ppermute | solution.py:108
  4.1 7.4 %collective-permute-start.1 = (bf16[64,768]{1,0:T(8,128)(2,1)}, bf16[64,768]{1,0:T(8,128)(2,1)S(1)}, u32[]{:S(2)}, u32[]{:S(2)}) collective-permute-start(bf16[64,768]{1,0:T(8,128)(2,1)} %refs_0_.1), channel_id=1, source_target_pairs={{0,2},{1,3},{2,0},{3,1},{4,6},{5,7},{6,4},{7,5},{8,10},{9,11},{10,... | collective-permute-start | bytes 294920 | tf_op jit(solution)/shard_map/ppermute | solution.py:108
  5.6 6.5 %collective-permute-start.2 = (bf16[64,768]{1,0:T(8,128)(2,1)}, bf16[64,768]{1,0:T(8,128)(2,1)S(1)}, u32[]{:S(2)}, u32[]{:S(2)}) collective-permute-start(bf16[64,768]{1,0:T(8,128)(2,1)} %refs_0_.1), channel_id=1, source_target_pairs={{0,4},{1,5},{2,6},{3,7},{4,0},{5,1},{6,2},{7,3},{8,12},{9,13},{10,... | collective-permute-start | bytes 294920 | tf_op jit(solution)/shard_map/ppermute | solution.py:108
  7.2 5.7 %collective-permute-start.3 = (bf16[64,768]{1,0:T(8,128)(2,1)}, bf16[64,768]{1,0:T(8,128)(2,1)S(1)}, u32[]{:S(2)}, u32[]{:S(2)}) collective-permute-start(bf16[64,768]{1,0:T(8,128)(2,1)} %refs_0_.1), channel_id=1, source_target_pairs={{0,6},{1,7},{2,4},{3,5},{4,2},{5,3},{6,0},{7,1},{8,14},{9,15},{10,... | collective-permute-start | bytes 294920 | tf_op jit(solution)/shard_map/ppermute | solution.py:108
  7.6 7.7 %collective-permute-start.7 = (bf16[64,768]{1,0:T(8,128)(2,1)}, bf16[64,768]{1,0:T(8,128)(2,1)S(1)}, u32[]{:S(2)}, u32[]{:S(2)}) collective-permute-start(bf16[64,768]{1,0:T(8,128)(2,1)} %refs_0_.1), channel_id=1, source_target_pairs={{0,1},{1,0},{2,3},{3,2},{4,5},{5,4},{6,7},{7,6},{8,9},{9,8},{10,11... | collective-permute-start | bytes 294920 | tf_op jit(solution)/shard_map/ppermute | solution.py:108
  8.3 0.7 %copy-start.6 = (s32[4]{0:T(128)S(1)}, s32[4]{0:T(128)}, u32[]{:S(2)}) copy-start(s32[4]{0:T(128)} %lengths_ref.1) | copy-start | bytes 52
  8.3 10.8 %copy-start = (bf16[12288,384]{1,0:T(8,128)(2,1)S(1)}, bf16[12288,384]{1,0:T(8,128)(2,1)}, u32[]{:S(2)}) copy-start(bf16[12288,384]{1,0:T(8,128)(2,1)} %refs_17_.1) | copy-start | bytes 28311556
  8.3 10.8 %copy-start.3 = (bf16[12288,64]{0,1:T(8,128)(2,1)S(1)}, bf16[12288,64]{0,1:T(8,128)(2,1)}, u32[]{:S(2)}) copy-start(bf16[12288,64]{0,1:T(8,128)(2,1)} %param.13) | copy-start | bytes 4718596
  8.3 10.8 %copy-start.4 = (bf16[64,768]{1,0:T(8,128)(2,1)S(1)}, bf16[64,768]{1,0:T(8,128)(2,1)}, u32[]{:S(2)}) copy-start(bf16[64,768]{1,0:T(8,128)(2,1)} %refs_0_.1) | copy-start | bytes 294916
  8.4 10.8 %copy-start.5 = (f32[12288]{0:T(1024)S(1)}, f32[12288]{0:T(1024)}, u32[]{:S(2)}) copy-start(f32[12288]{0:T(1024)} %param.11) | copy-start | bytes 147460
  8.4 36.6 %slice-start = ((s8[9437184]{0:T(1024)(128)(4,1)}), s8[4194304]{0:T(1024)(128)(4,1)S(1)}, s32[]{:S(2)}) async-start(s8[9437184]{0:T(1024)(128)(4,1)} %bitcast.38), calls=%async_computation.2 | async-start | bytes 8388608
  8.4 36.6 %slice-start.1 = ((s8[9437184]{0:T(1024)(128)(4,1)}), s8[4194304]{0:T(1024)(128)(4,1)S(1)}, s32[]{:S(2)}) async-start(s8[9437184]{0:T(1024)(128)(4,1)} %bitcast.38), calls=%async_computation.3 | async-start | bytes 8388608
  9.3 5.9 %collective-permute-start.6 = (bf16[64,768]{1,0:T(8,128)(2,1)S(1)}, bf16[64,768]{1,0:T(8,128)(2,1)S(1)}, u32[]{:S(2)}, u32[]{:S(2)}) collective-permute-start(bf16[64,768]{1,0:T(8,128)(2,1)S(1)} %collective-permute-done.refs_1_), channel_id=1, source_target_pairs={{0,6},{1,7},{2,4},{3,5},{4,2},{5,3},{6,0},{7,1},{8,14},{9,15},{10,... | collective-permute-start | bytes 294920 | tf_op jit(solution)/shard_map/ppermute | solution.py:108
  11.5 5.7 %collective-permute-start.4 = (bf16[64,768]{1,0:T(8,128)(2,1)S(1)}, bf16[64,768]{1,0:T(8,128)(2,1)S(1)}, u32[]{:S(2)}, u32[]{:S(2)}) collective-permute-start(bf16[64,768]{1,0:T(8,128)(2,1)S(1)} %collective-permute-done.refs_1_), channel_id=1, source_target_pairs={{0,2},{1,3},{2,0},{3,1},{4,6},{5,7},{6,4},{7,5},{8,10},{9,11},{10,... | collective-permute-start | bytes 294920 | tf_op jit(solution)/shard_map/ppermute | solution.py:108
  12.1 5.1 %collective-permute-start.5 = (bf16[64,768]{1,0:T(8,128)(2,1)S(1)}, bf16[64,768]{1,0:T(8,128)(2,1)S(1)}, u32[]{:S(2)}, u32[]{:S(2)}) collective-permute-start(bf16[64,768]{1,0:T(8,128)(2,1)S(1)} %collective-permute-done.refs_1_), channel_id=1, source_target_pairs={{0,4},{1,5},{2,6},{3,7},{4,0},{5,1},{6,2},{7,3},{8,12},{9,13},{10,... | collective-permute-start | bytes 294920 | tf_op jit(solution)/shard_map/ppermute | solution.py:108
  12.9 4.8 %collective-permute-start.8 = (bf16[64,768]{1,0:T(8,128)(2,1)S(1)}, bf16[64,768]{1,0:T(8,128)(2,1)S(1)}, u32[]{:S(2)}, u32[]{:S(2)}) collective-permute-start(bf16[64,768]{1,0:T(8,128)(2,1)S(1)} %collective-permute-done.refs_1_), channel_id=1, source_target_pairs={{0,1},{1,0},{2,3},{3,2},{4,5},{5,4},{6,7},{7,6},{8,9},{9,8},{10,11... | collective-permute-start | bytes 294920 | tf_op jit(solution)/shard_map/ppermute | solution.py:108
  15.1 2.6 %collective-permute-start.14 = (bf16[64,768]{1,0:T(8,128)(2,1)S(1)}, bf16[64,768]{1,0:T(8,128)(2,1)S(1)}, u32[]{:S(2)}, u32[]{:S(2)}) collective-permute-start(bf16[64,768]{1,0:T(8,128)(2,1)S(1)} %collective-permute-done.6.refs_7_), channel_id=1, source_target_pairs={{0,1},{1,0},{2,3},{3,2},{4,5},{5,4},{6,7},{7,6},{8,9},{9,8},{10,11... | collective-permute-start | bytes 294920 | tf_op jit(solution)/shard_map/ppermute | solution.py:108
  15.3 3.0 %collective-permute-start.9 = (bf16[64,768]{1,0:T(8,128)(2,1)S(1)}, bf16[64,768]{1,0:T(8,128)(2,1)S(1)}, u32[]{:S(2)}, u32[]{:S(2)}) collective-permute-start(bf16[64,768]{1,0:T(8,128)(2,1)S(1)} %collective-permute-done.1.refs_2_), channel_id=1, source_target_pairs={{0,1},{1,0},{2,3},{3,2},{4,5},{5,4},{6,7},{7,6},{8,9},{9,8},{10,11... | collective-permute-start | bytes 294920 | tf_op jit(solution)/shard_map/ppermute | solution.py:108
  17.2 1.3 %collective-permute-start.10 = (bf16[64,768]{1,0:T(8,128)(2,1)S(1)}, bf16[64,768]{1,0:T(8,128)(2,1)S(1)}, u32[]{:S(2)}, u32[]{:S(2)}) collective-permute-start(bf16[64,768]{1,0:T(8,128)(2,1)S(1)} %collective-permute-done.2.refs_3_), channel_id=1, source_target_pairs={{0,1},{1,0},{2,3},{3,2},{4,5},{5,4},{6,7},{7,6},{8,9},{9,8},{10,11... | collective-permute-start | bytes 294920 | tf_op jit(solution)/shard_map/ppermute | solution.py:108
  17.2 1.4 %collective-permute-start.11 = (bf16[64,768]{1,0:T(8,128)(2,1)S(1)}, bf16[64,768]{1,0:T(8,128)(2,1)S(1)}, u32[]{:S(2)}, u32[]{:S(2)}) collective-permute-start(bf16[64,768]{1,0:T(8,128)(2,1)S(1)} %collective-permute-done.3.refs_4_), channel_id=1, source_target_pairs={{0,1},{1,0},{2,3},{3,2},{4,5},{5,4},{6,7},{7,6},{8,9},{9,8},{10,11... | collective-permute-start | bytes 294920 | tf_op jit(solution)/shard_map/ppermute | solution.py:108
  17.7 1.3 %collective-permute-start.12 = (bf16[64,768]{1,0:T(8,128)(2,1)S(1)}, bf16[64,768]{1,0:T(8,128)(2,1)S(1)}, u32[]{:S(2)}, u32[]{:S(2)}) collective-permute-start(bf16[64,768]{1,0:T(8,128)(2,1)S(1)} %collective-permute-done.4.refs_5_), channel_id=1, source_target_pairs={{0,1},{1,0},{2,3},{3,2},{4,5},{5,4},{6,7},{7,6},{8,9},{9,8},{10,11... | collective-permute-start | bytes 294920 | tf_op jit(solution)/shard_map/ppermute | solution.py:108
  17.8 1.4 %collective-permute-start.13 = (bf16[64,768]{1,0:T(8,128)(2,1)S(1)}, bf16[64,768]{1,0:T(8,128)(2,1)S(1)}, u32[]{:S(2)}, u32[]{:S(2)}) collective-permute-start(bf16[64,768]{1,0:T(8,128)(2,1)S(1)} %collective-permute-done.5.refs_6_), channel_id=1, source_target_pairs={{0,1},{1,0},{2,3},{3,2},{4,5},{5,4},{6,7},{7,6},{8,9},{9,8},{10,11... | collective-permute-start | bytes 294920 | tf_op jit(solution)/shard_map/ppermute | solution.py:108
  19.2 14.5 %copy-start.1 = (bf16[4,512,512]{2,1,0:T(8,128)(2,1)S(1)}, bf16[4,512,512]{2,1,0:T(8,128)(2,1)}, u32[]{:S(2)}) copy-start(bf16[4,512,512]{2,1,0:T(8,128)(2,1)} %keys_ref.1) | copy-start | bytes 6291460
  19.2 14.5 %copy-start.2 = (bf16[4,512,512]{2,1,0:T(8,128)(2,1)S(1)}, bf16[4,512,512]{2,1,0:T(8,128)(2,1)}, u32[]{:S(2)}) copy-start(bf16[4,512,512]{2,1,0:T(8,128)(2,1)} %values_ref.1) | copy-start | bytes 6291460
  19.2 25.8 %slice-start.2 = ((s8[9437184]{0:T(1024)(128)(4,1)}), s8[1048576]{0:T(1024)(128)(4,1)S(1)}, s32[]{:S(2)}) async-start(s8[9437184]{0:T(1024)(128)(4,1)} %bitcast.38), calls=%async_computation.4 | async-start | bytes 2097152
  45.6 2.4 %collective-permute-start.19 = (bf16[4,64,768]{2,1,0:T(8,128)(2,1)S(1)}, bf16[4,64,768]{2,1,0:T(8,128)(2,1)S(1)}, u32[]{:S(2)}, u32[]{:S(2)}) collective-permute-start(bf16[4,64,768]{2,1,0:T(8,128)(2,1)S(1)} %expand.7), channel_id=1, source_target_pairs={{0,1},{1,0},{2,3},{3,2},{4,5},{5,4},{6,7},{7,6},{8,9},{9,8},{10,11... | collective-permute-start | bytes 1179656 | tf_op jit(solution)/shard_map/ppermute | solution.py:108
  46.2 5.3 %collective-permute-start.15 = (bf16[4,64,768]{2,1,0:T(8,128)(2,1)S(1)}, bf16[4,64,768]{2,1,0:T(8,128)(2,1)S(1)}, u32[]{:S(2)}, u32[]{:S(2)}) collective-permute-start(bf16[4,64,768]{2,1,0:T(8,128)(2,1)S(1)} %expand.5), channel_id=1, source_target_pairs={{0,1},{1,0},{2,3},{3,2},{4,5},{5,4},{6,7},{7,6},{8,9},{9,8},{10,11... | collective-permute-start | bytes 1179656 | tf_op jit(solution)/shard_map/ppermute | solution.py:108
  48.0 4.8 %collective-permute-start.22 = (bf16[64,768]{1,0:T(8,128)(2,1)S(1)}, bf16[64,768]{1,0:T(8,128)(2,1)S(1)}, u32[]{:S(2)}, u32[]{:S(2)}) collective-permute-start(bf16[64,768]{1,0:T(8,128)(2,1)S(1)} %get-tuple-element.23), channel_id=1, source_target_pairs={{0,2},{1,3},{2,0},{3,1},{4,6},{5,7},{6,4},{7,5},{8,10},{9,11},{10,... | collective-permute-start | bytes 294920 | tf_op jit(solution)/shard_map/ppermute | solution.py:108
  48.3 6.9 %collective-permute-start.21 = (bf16[64,768]{1,0:T(8,128)(2,1)S(1)}, bf16[64,768]{1,0:T(8,128)(2,1)S(1)}, u32[]{:S(2)}, u32[]{:S(2)}) collective-permute-start(bf16[64,768]{1,0:T(8,128)(2,1)S(1)} %get-tuple-element.24), channel_id=1, source_target_pairs={{0,4},{1,5},{2,6},{3,7},{4,0},{5,1},{6,2},{7,3},{8,12},{9,13},{10,... | collective-permute-start | bytes 294920 | tf_op jit(solution)/shard_map/ppermute | solution.py:108
  48.9 8.5 %collective-permute-start.20 = (bf16[64,768]{1,0:T(8,128)(2,1)S(1)}, bf16[64,768]{1,0:T(8,128)(2,1)S(1)}, u32[]{:S(2)}, u32[]{:S(2)}) collective-permute-start(bf16[64,768]{1,0:T(8,128)(2,1)S(1)} %get-tuple-element.22), channel_id=1, source_target_pairs={{0,6},{1,7},{2,4},{3,5},{4,2},{5,3},{6,0},{7,1},{8,14},{9,15},{10,... | collective-permute-start | bytes 294920 | tf_op jit(solution)/shard_map/ppermute | solution.py:108
  51.6 6.2 %collective-permute-start.18 = (bf16[64,768]{1,0:T(8,128)(2,1)S(1)}, bf16[64,768]{1,0:T(8,128)(2,1)S(1)}, u32[]{:S(2)}, u32[]{:S(2)}) collective-permute-start(bf16[64,768]{1,0:T(8,128)(2,1)S(1)} %get-tuple-element.20), channel_id=1, source_target_pairs={{0,2},{1,3},{2,0},{3,1},{4,6},{5,7},{6,4},{7,5},{8,10},{9,11},{10,... | collective-permute-start | bytes 294920 | tf_op jit(solution)/shard_map/ppermute | solution.py:108
  51.9 6.2 %collective-permute-start.17 = (bf16[64,768]{1,0:T(8,128)(2,1)S(1)}, bf16[64,768]{1,0:T(8,128)(2,1)S(1)}, u32[]{:S(2)}, u32[]{:S(2)}) collective-permute-start(bf16[64,768]{1,0:T(8,128)(2,1)S(1)} %get-tuple-element.21), channel_id=1, source_target_pairs={{0,4},{1,5},{2,6},{3,7},{4,0},{5,1},{6,2},{7,3},{8,12},{9,13},{10,... | collective-permute-start | bytes 294920 | tf_op jit(solution)/shard_map/ppermute | solution.py:108
  52.8 8.6 %collective-permute-start.16 = (bf16[64,768]{1,0:T(8,128)(2,1)S(1)}, bf16[64,768]{1,0:T(8,128)(2,1)S(1)}, u32[]{:S(2)}, u32[]{:S(2)}) collective-permute-start(bf16[64,768]{1,0:T(8,128)(2,1)S(1)} %get-tuple-element.19), channel_id=1, source_target_pairs={{0,6},{1,7},{2,4},{3,5},{4,2},{5,3},{6,0},{7,1},{8,14},{9,15},{10,... | collective-permute-start | bytes 294920 | tf_op jit(solution)/shard_map/ppermute | solution.py:108
  57.5 6.1 %collective-permute-start.23 = (bf16[64,768]{1,0:T(8,128)(2,1)S(1)}, bf16[64,768]{1,0:T(8,128)(2,1)S(1)}, u32[]{:S(2)}, u32[]{:S(2)}) collective-permute-start(bf16[64,768]{1,0:T(8,128)(2,1)S(1)} %fusion.7), channel_id=1, source_target_pairs={{0,8},{1,9},{2,10},{3,11},{4,12},{5,13},{6,14},{7,15},{8,0},{9,1},... | collective-permute-start | bytes 294920 | tf_op jit(solution)/shard_map/ppermute | solution.py:108
where the time goes:
time: 64.7 us; the launch traced here: 64.4 us
  blocking collectives  21.3 us (33%)
  starting transfers between devices  20.6 us (32%)
  waiting for transfers between devices  13.1 us (20%)
  Pallas kernels  6.75 us (10%)
  other arithmetic  1.84 us (3%)
    ppermute x24, starting transfers between devices, swapped(): return lax.ppermute(value, 'out', [(i, i ^ mask) for i in range(size)])  20.6 us
    ppermute x24, waiting for transfers between devices, swapped(): return lax.ppermute(value, 'out', [(i, i ^ mask) for i in range(size)])  13.1 us
    all_to_all x1, blocking collectives, per_device(): rows = lax.all_to_all(qkv, 'out', split_axis=0, concat_axis=0, tiled=True)  11.9 us
    all_to_all x1, blocking collectives, per_device(): lax.all_to_all(attended, 'out', split_axis=0, concat_axis=0, tiled=True)  9.34 us
    pallas_call x1, Pallas kernels, project(): pl.pallas_call(lambda *refs: project_kernel(order, pieces, *refs), out_sh...  2.53 us
    pallas_call x4, Pallas kernels, expand(): pl.pallas_call(lambda *refs: expand_kernel(order, *refs), out_shape=jax.S...  2.29 us
    pallas_call x1, Pallas kernels, attend(): pl.pallas_call(attend_kernel, out_shape=jax.ShapeDtypeStruct((sources, lo...  1.92 us
  transfers between devices with their start and end apart: 24, of which 12 were waited for; matrix products, arithmetic and copies ran while one was open for 2% of the time, Pallas kernels for 3%

commit v1 on v0

--- a/solution.py
+++ b/solution.py
@@ -137,19 +137,40 @@
     )(*[room] * count)
 
 
-def project_kernel(order, pieces, *refs):
+def squares(refs):
+    total = jnp.zeros((refs[0].shape[0], 128), jnp.float32)
+    for ref in refs:
+        part = ref[...].astype(jnp.float32)
+        part = part * part
+        for lane in range(0, part.shape[1], 128):
+            total += part[:, lane : lane + 128]
+    return total
+
+
+def early_squares_kernel(*refs):
+    refs[-1][...] = squares(refs[:-1])
+
+
+def early_squares(shards):
+    vmem = pl.BlockSpec(memory_space=pltpu.VMEM)
+    return pl.pallas_call(
+        early_squares_kernel,
+        out_shape=jax.ShapeDtypeStruct((shards[0].shape[0], 128), jnp.float32),
+        in_specs=[vmem] * len(shards),
+        out_specs=vmem,
+        compiler_params=pltpu.CompilerParams(vmem_limit_bytes=2 * 1024 * 1024),
+        name="early_squares",
+    )(*shards)
+
+
+def project_kernel(order, pieces, late, *refs):
     shards = refs[:pieces]
-    gain_ref, wq_ref, wkv_ref, _, out_ref = refs[pieces:]
+    gain_ref, wq_ref, wkv_ref, _, early_ref, out_ref = refs[pieces:]
     rows, depth = shards[0].shape
     columns, kv_columns = wq_ref.shape[1], wkv_ref.shape[0]
     targets, per_target, _ = out_ref.shape
     me = lax.axis_index("out")
-    square = jnp.zeros((rows, 128), jnp.float32)
-    for k in range(pieces):
-        part = shards[k][...].astype(jnp.float32)
-        part = part * part
-        for lane in range(0, depth, 128):
-            square += part[:, lane : lane + 128]
+    square = early_ref[...] + squares([shards[k] for k in late])
     meansq = jnp.sum(square, axis=-1, keepdims=True) / (depth * pieces)
     inverse = lax.rsqrt(meansq + norm_eps)
     q_sum = jnp.zeros((rows, columns), jnp.float32)
@@ -173,20 +194,20 @@
         out_ref[k, :, columns:] = both[take].astype(jnp.bfloat16)
 
 
-def project(order, shards, norm_gain, w_query, w_keyval, mark, per_target):
+def project(order, late, shards, early, norm_gain, w_query, w_keyval, mark, per_target):
     pieces = len(shards)
     rows = shards[0].shape[0]
     vmem = pl.BlockSpec(memory_space=pltpu.VMEM)
     return pl.pallas_call(
-        lambda *refs: project_kernel(order, pieces, *refs),
+        lambda *refs: project_kernel(order, pieces, late, *refs),
         out_shape=jax.ShapeDtypeStruct(
             (rows // per_target, per_target, w_query.shape[1] + 2 * w_keyval.shape[0]), jnp.bfloat16
         ),
-        in_specs=[vmem] * (pieces + 4),
+        in_specs=[vmem] * (pieces + 5),
         out_specs=vmem,
         compiler_params=pltpu.CompilerParams(vmem_limit_bytes=16 * 1024 * 1024),
         name="project",
-    )(*shards, norm_gain, w_query, w_keyval, mark)
+    )(*shards, norm_gain, w_query, w_keyval, mark, early)
 
 
 def attend_kernel(
@@ -360,7 +381,10 @@
         jnp.exp2(value_scales.astype(jnp.float32)),
     )
     side, held[size - 1] = lax.optimization_barrier((side, held[size - 1]))
-    qkv = project(order, [held[m] for m in order], norm_gain, w_query, w_keyval, mark, local_rows)
+    late = [k for k, m in enumerate(order) if m > size // 2 and m & 1]
+    early = early_squares([held[m] for k, m in enumerate(order) if k not in late])
+    shards = [held[m] for m in order]
+    qkv = project(order, late, shards, early, norm_gain, w_query, w_keyval, mark, local_rows)
     rows = lax.all_to_all(qkv, "out", split_axis=0, concat_axis=0, tiled=True)
     attended = attend(rows, columns, lengths, *side, key_cache, value_cache)
     heads = lax.all_to_all(attended, "out", split_axis=0, concat_axis=0, tiled=True)

time: 64.7 us -> 65 us (level)
  other arithmetic: 1.84 us -> 1.13 us
  waiting for transfers between devices: 13.1 us -> 13.8 us
    exp2 x1, other arithmetic: 0.73 us -> 0.01 us  [per_device(): jnp.exp2(value_scales.astype(jnp.float32))]
    ppermute x24, waiting for transfers between devices: 13.1 us -> 13.8 us  [swapped(): return lax.ppermute(value, 'out', [(i, i ^ mask) for i in range(size)])]
    pallas_call x1 -> x2, Pallas kernels: 2.53 us -> 2.53 us  [the longest x1 2.26 us: project(): pl.pallas_call(lambda *refs: project_kernel(order, pieces, late, *refs),...]
  transfers between devices with their start and end apart: 24 -> 24, of which waited for: 12 -> 10; matrix products, arithmetic and copies ran while one was open for 2% -> 1% of each run, Pallas kernels for 3% -> 3%
where the time goes in v1:
time: 65 us; the launch traced here: 64.8 us
  blocking collectives  21.8 us (34%)
  starting transfers between devices  20.2 us (31%)
  waiting for transfers between devices  13.8 us (21%)
  Pallas kernels  6.74 us (10%)
  other arithmetic  1.13 us (2%)
  local copies, waits for them, and re-layouts  0.84 us (1%)
    ppermute x24, starting transfers between devices, swapped(): return lax.ppermute(value, 'out', [(i, i ^ mask) for i in range(size)])  20.2 us
    ppermute x24, waiting for transfers between devices, swapped(): return lax.ppermute(value, 'out', [(i, i ^ mask) for i in range(size)])  13.8 us
    all_to_all x1, blocking collectives, per_device(): rows = lax.all_to_all(qkv, 'out', split_axis=0, concat_axis=0, tiled=True)  12.5 us
    all_to_all x1, blocking collectives, per_device(): lax.all_to_all(attended, 'out', split_axis=0, concat_axis=0, tiled=True)  9.34 us
    pallas_call x4, Pallas kernels, expand(): pl.pallas_call(lambda *refs: expand_kernel(order, *refs), out_shape=jax.S...  2.29 us
    pallas_call x1, Pallas kernels, project(): pl.pallas_call(lambda *refs: project_kernel(order, pieces, late, *refs),...  2.26 us
    pallas_call x1, Pallas kernels, attend(): pl.pallas_call(attend_kernel, out_shape=jax.ShapeDtypeStruct((sources, lo...  1.92 us
  transfers between devices with their start and end apart: 24, of which 10 were waited for; matrix products, arithmetic and copies ran while one was open for 1% of the time, Pallas kernels for 3%

profile of v1, /device:TPU:0, one launch (start us, length us, event | category | flops | bytes accessed | tf_op | source)
XLA Modules:
  0.0 64.8 jit_solution(4516187474762188617)
XLA Ops:
  0.0 4.1 %collective-permute-start = (bf16[64,768]{1,0:T(8,128)(2,1)}, bf16[64,768]{1,0:T(8,128)(2,1)S(1)}, u32[]{:S(2)}, u32[]{:S(2)}) collective-permute-start(bf16[64,768]{1,0:T(8,128)(2,1)} %refs_0_.3), channel_id=1, source_target_pairs={{0,8},{1,9},{2,10},{3,11},{4,12},{5,13},{6,14},{7,15},{8,0},{9,1},... | collective-permute-start | bytes 294920 | tf_op jit(solution)/shard_map/ppermute | solution.py:108
  4.1 1.5 %collective-permute-start.1 = (bf16[64,768]{1,0:T(8,128)(2,1)}, bf16[64,768]{1,0:T(8,128)(2,1)S(1)}, u32[]{:S(2)}, u32[]{:S(2)}) collective-permute-start(bf16[64,768]{1,0:T(8,128)(2,1)} %refs_0_.3), channel_id=1, source_target_pairs={{0,2},{1,3},{2,0},{3,1},{4,6},{5,7},{6,4},{7,5},{8,10},{9,11},{10,... | collective-permute-start | bytes 294920 | tf_op jit(solution)/shard_map/ppermute | solution.py:108
  5.6 1.6 %collective-permute-start.2 = (bf16[64,768]{1,0:T(8,128)(2,1)}, bf16[64,768]{1,0:T(8,128)(2,1)S(1)}, u32[]{:S(2)}, u32[]{:S(2)}) collective-permute-start(bf16[64,768]{1,0:T(8,128)(2,1)} %refs_0_.3), channel_id=1, source_target_pairs={{0,4},{1,5},{2,6},{3,7},{4,0},{5,1},{6,2},{7,3},{8,12},{9,13},{10,... | collective-permute-start | bytes 294920 | tf_op jit(solution)/shard_map/ppermute | solution.py:108
  7.2 0.4 collective-permute-start.3
  7.6 0.0 collective-permute-start.7
  7.6 0.0 copy-start.6
  7.6 0.0 copy-start.7
  7.6 0.0 copy-start.3
  7.6 0.0 slice-start.4
  7.6 0.0 slice-start.5
  7.6 0.0 copy-start.2
  7.6 0.0 copy-start.4
  7.7 0.7 %copy-done.5 = s32[4]{0:T(128)S(1)} copy-done((s32[4]{0:T(128)S(1)}, s32[4]{0:T(128)}, u32[]{:S(2)}) %copy-start.5) | copy-done | bytes 40
  8.4 0.1 copy-done.6
  8.4 0.0 copy-done.7
  8.5 0.8 %collective-permute-done.refs_1_ = bf16[64,768]{1,0:T(8,128)(2,1)S(1)} collective-permute-done((bf16[64,768]{1,0:T(8,128)(2,1)}, bf16[64,768]{1,0:T(8,128)(2,1)S(1)}, u32[]{:S(2)}, u32[]{:S(2)}) %collective-permute-start) | collective-permute-done | bytes 98336 | tf_op jit(solution)/shard_map/ppermute | solution.py:108
  9.3 1.4 %collective-permute-start.4 = (bf16[64,768]{1,0:T(8,128)(2,1)S(1)}, bf16[64,768]{1,0:T(8,128)(2,1)S(1)}, u32[]{:S(2)}, u32[]{:S(2)}) collective-permute-start(bf16[64,768]{1,0:T(8,128)(2,1)S(1)} %collective-permute-done.refs_1_), channel_id=1, source_target_pairs={{0,2},{1,3},{2,0},{3,1},{4,6},{5,7},{6,4},{7,5},{8,10},{9,11},{10,... | collective-permute-start | bytes 294920 | tf_op jit(solution)/shard_map/ppermute | solution.py:108
  10.7 0.0 collective-permute-done.1.refs_2_
  10.7 0.9 %collective-permute-start.5 = (bf16[64,768]{1,0:T(8,128)(2,1)S(1)}, bf16[64,768]{1,0:T(8,128)(2,1)S(1)}, u32[]{:S(2)}, u32[]{:S(2)}) collective-permute-start(bf16[64,768]{1,0:T(8,128)(2,1)S(1)} %collective-permute-done.refs_1_), channel_id=1, source_target_pairs={{0,4},{1,5},{2,6},{3,7},{4,0},{5,1},{6,2},{7,3},{8,12},{9,13},{10,... | collective-permute-start | bytes 294920 | tf_op jit(solution)/shard_map/ppermute | solution.py:108
  11.6 0.0 collective-permute-done.2.refs_3_
  11.7 1.3 %collective-permute-start.6 = (bf16[64,768]{1,0:T(8,128)(2,1)S(1)}, bf16[64,768]{1,0:T(8,128)(2,1)S(1)}, u32[]{:S(2)}, u32[]{:S(2)}) collective-permute-start(bf16[64,768]{1,0:T(8,128)(2,1)S(1)} %collective-permute-done.refs_1_), channel_id=1, source_target_pairs={{0,6},{1,7},{2,4},{3,5},{4,2},{5,3},{6,0},{7,1},{8,14},{9,15},{10,... | collective-permute-start | bytes 294920 | tf_op jit(solution)/shard_map/ppermute | solution.py:108
  13.0 0.0 collective-permute-done.3.refs_4_
  13.0 0.0 collective-permute-start.9
  13.0 0.0 collective-permute-done.7.refs_8_
  13.0 0.5 collective-permute-start.10
  13.5 0.1 fusion.24
  13.6 1.4 %collective-permute-done.4.refs_5_ = bf16[64,768]{1,0:T(8,128)(2,1)S(1)} collective-permute-done((bf16[64,768]{1,0:T(8,128)(2,1)S(1)}, bf16[64,768]{1,0:T(8,128)(2,1)S(1)}, u32[]{:S(2)}, u32[]{:S(2)}) %collective-permute-start.4) | collective-permute-done | bytes 98336 | tf_op jit(solution)/shard_map/ppermute | solution.py:108
  15.0 0.0 collective-permute-start.8
  15.0 1.2 %collective-permute-done.5.refs_6_ = bf16[64,768]{1,0:T(8,128)(2,1)S(1)} collective-permute-done((bf16[64,768]{1,0:T(8,128)(2,1)S(1)}, bf16[64,768]{1,0:T(8,128)(2,1)S(1)}, u32[]{:S(2)}, u32[]{:S(2)}) %collective-permute-start.5) | collective-permute-done | bytes 98336 | tf_op jit(solution)/shard_map/ppermute | solution.py:108
  16.2 1.2 %collective-permute-done.6.refs_7_ = bf16[64,768]{1,0:T(8,128)(2,1)S(1)} collective-permute-done((bf16[64,768]{1,0:T(8,128)(2,1)S(1)}, bf16[64,768]{1,0:T(8,128)(2,1)S(1)}, u32[]{:S(2)}, u32[]{:S(2)}) %collective-permute-start.6) | collective-permute-done | bytes 98336 | tf_op jit(solution)/shard_map/ppermute | solution.py:108
  17.5 0.5 collective-permute-start.13
  18.0 0.1 collective-permute-start.14
  18.1 0.1 pad_maximum_fusion
  18.1 0.3 early_squares.1.refs_20_
  18.4 0.9 %collective-permute-done.14.refs_15_ = bf16[64,768]{1,0:T(8,128)(2,1)S(1)} collective-permute-done((bf16[64,768]{1,0:T(8,128)(2,1)S(1)}, bf16[64,768]{1,0:T(8,128)(2,1)S(1)}, u32[]{:S(2)}, u32[]{:S(2)}) %collective-permute-start.14) | collective-permute-done | bytes 98336 | tf_op jit(solution)/shard_map/ppermute | solution.py:108
  19.4 0.0 copy-start
  19.4 0.0 copy-start.1
  19.4 0.0 slice-start.1
  19.4 2.3 %project.1 = bf16[16,4,512]{2,1,0:T(4,128)(2,1)S(1)} custom-call(bf16[64,768]{1,0:T(8,128)(2,1)S(1)} %copy-done.3, bf16[64,768]{1,0:T(8,128)(2,1)S(1)} %collective-permute-done.refs_1_, bf16[64,768]{1,0:T(8,128)(2,1)S(1)} %collective-permute-done.1.refs_2_, bf16[64,768]{1,0:T(8,128)(2,1)S(1)} %collective-permute-done.2.refs_3_, ...), custom_call_target="tpu_custom_call" | custom-call | tf_op jit(solution)/shard_map/project/pallas_call | solution.py:201
  21.7 12.5 %all_to_all.10.rows_ref = bf16[16,4,512]{2,1,0:T(4,128)(2,1)S(1)} all-to-all(bf16[16,4,512]{2,1,0:T(4,128)(2,1)S(1)} %project.1), channel_id=1, replica_groups=mesh['groups'=2,'out'=16] {'out'}, dimensions={0} | all-to-all | bytes 131072 | tf_op jit(solution)/shard_map/all_to_all | solution.py:388
  34.1 1.9 %attend.1 = bf16[16,4,384]{2,1,0:T(4,128)(2,1)S(1)} custom-call(s32[4]{0:T(128)S(1)} %copy-done.5, bf16[16,4,512]{2,1,0:T(4,128)(2,1)S(1)} %all_to_all.10.rows_ref, f32[4,128]{1,0:T(4,128)S(1)} %get-tuple-element.15.cos_ref, f32[4,128]{1,0:T(4,128)S(1)} %get-tuple-element.16.sin_ref, f32[4,4,4]{2,1,0:T(4,128)S(1)} %get-tuple-element.17.kf_ref, ...), custom_call_target="tpu_custom_call" | custom-call | tf_op jit(solution)/shard_map/attend/pallas_call | solution.py:300
  36.1 9.3 %all_to_all.11.refs_0_ = bf16[16,4,384]{2,1,0:T(4,128)(2,1)S(1)} all-to-all(bf16[16,4,384]{2,1,0:T(4,128)(2,1)S(1)} %attend.1), channel_id=1, replica_groups=mesh['groups'=2,'out'=16] {'out'}, dimensions={0} | all-to-all | bytes 98304 | tf_op jit(solution)/shard_map/all_to_all | solution.py:390
  45.4 0.6 expand.7
  46.0 0.1 collective-permute-start.19
  46.1 0.6 expand.5
  46.7 0.6 collective-permute-start.15
  47.2 0.6 expand.4
  47.8 0.6 expand.6
  48.4 0.1 fusion.21
  48.5 0.3 collective-permute-start.22
  48.8 0.6 collective-permute-start.21
  49.4 2.6 %collective-permute-start.20 = (bf16[64,768]{1,0:T(8,128)(2,1)S(1)}, bf16[64,768]{1,0:T(8,128)(2,1)S(1)}, u32[]{:S(2)}, u32[]{:S(2)}) collective-permute-start(bf16[64,768]{1,0:T(8,128)(2,1)S(1)} %get-tuple-element.22), channel_id=1, source_target_pairs={{0,6},{1,7},{2,4},{3,5},{4,2},{5,3},{6,0},{7,1},{8,14},{9,15},{10,... | collective-permute-start | bytes 294920 | tf_op jit(solution)/shard_map/ppermute | solution.py:108
  52.0 0.1 fusion.18
  52.1 0.3 collective-permute-start.18
  52.4 0.6 collective-permute-start.17
  53.0 0.3 collective-permute-done.22
  53.3 2.4 %collective-permute-start.16 = (bf16[64,768]{1,0:T(8,128)(2,1)S(1)}, bf16[64,768]{1,0:T(8,128)(2,1)S(1)}, u32[]{:S(2)}, u32[]{:S(2)}) collective-permute-start(bf16[64,768]{1,0:T(8,128)(2,1)S(1)} %get-tuple-element.19), channel_id=1, source_target_pairs={{0,6},{1,7},{2,4},{3,5},{4,2},{5,3},{6,0},{7,1},{8,14},{9,15},{10,... | collective-permute-start | bytes 294920 | tf_op jit(solution)/shard_map/ppermute | solution.py:108
  55.7 2.2 %collective-permute-done.20 = bf16[64,768]{1,0:T(8,128)(2,1)S(1)} collective-permute-done((bf16[64,768]{1,0:T(8,128)(2,1)S(1)}, bf16[64,768]{1,0:T(8,128)(2,1)S(1)}, u32[]{:S(2)}, u32[]{:S(2)}) %collective-permute-start.20) | collective-permute-done | bytes 98336 | tf_op jit(solution)/shard_map/ppermute | solution.py:108
  57.9 0.1 fusion.7
  57.9 0.4 collective-permute-start.23
  58.3 0.3 collective-permute-done.17
  58.6 3.2 %collective-permute-done.16 = bf16[64,768]{1,0:T(8,128)(2,1)S(1)} collective-permute-done((bf16[64,768]{1,0:T(8,128)(2,1)S(1)}, bf16[64,768]{1,0:T(8,128)(2,1)S(1)}, u32[]{:S(2)}, u32[]{:S(2)}) %collective-permute-start.16) | collective-permute-done | bytes 98336 | tf_op jit(solution)/shard_map/ppermute | solution.py:108
  61.8 2.3 %collective-permute-done.23 = bf16[64,768]{1,0:T(8,128)(2,1)S(1)} collective-permute-done((bf16[64,768]{1,0:T(8,128)(2,1)S(1)}, bf16[64,768]{1,0:T(8,128)(2,1)S(1)}, u32[]{:S(2)}, u32[]{:S(2)}) %collective-permute-start.23) | collective-permute-done | bytes 98336 | tf_op jit(solution)/shard_map/ppermute | solution.py:108
  64.1 0.7 %fusion.17 = bf16[64,768]{1,0:T(8,128)(2,1)} fusion(f32[4,64,768]{2,1,0:T(8,128)S(1)} %expand.4, bf16[64,768]{1,0:T(8,128)(2,1)S(1)} %collective-permute-done.23, bf16[64,768]{1,0:T(8,128)(2,1)S(1)} %collective-permute-done.18, bf16[64,768]{1,0:T(8,128)(2,1)S(1)} %collective-permute-done.17, bf16[64,768]{1,0:T(8,128)(2,1)S(1)} %collective-permute-done.16, ...), kind=kLoop, calls=%fused_computation.25 | loop fusion | flops 638976 | bytes 884736 | tf_op jit(solution)/shard_map/convert_element_type | solution.py:409
  (34 shorter events, 0.1 us)
Async XLA Ops:
  0.0 9.3 %collective-permute-start = (bf16[64,768]{1,0:T(8,128)(2,1)}, bf16[64,768]{1,0:T(8,128)(2,1)S(1)}, u32[]{:S(2)}, u32[]{:S(2)}) collective-permute-start(bf16[64,768]{1,0:T(8,128)(2,1)} %refs_0_.3), channel_id=1, source_target_pairs={{0,8},{1,9},{2,10},{3,11},{4,12},{5,13},{6,14},{7,15},{8,0},{9,1},... | collective-permute-start | bytes 294920 | tf_op jit(solution)/shard_map/ppermute | solution.py:108
  4.1 6.6 %collective-permute-start.1 = (bf16[64,768]{1,0:T(8,128)(2,1)}, bf16[64,768]{1,0:T(8,128)(2,1)S(1)}, u32[]{:S(2)}, u32[]{:S(2)}) collective-permute-start(bf16[64,768]{1,0:T(8,128)(2,1)} %refs_0_.3), channel_id=1, source_target_pairs={{0,2},{1,3},{2,0},{3,1},{4,6},{5,7},{6,4},{7,5},{8,10},{9,11},{10,... | collective-permute-start | bytes 294920 | tf_op jit(solution)/shard_map/ppermute | solution.py:108
  5.6 6.1 %collective-permute-start.2 = (bf16[64,768]{1,0:T(8,128)(2,1)}, bf16[64,768]{1,0:T(8,128)(2,1)S(1)}, u32[]{:S(2)}, u32[]{:S(2)}) collective-permute-start(bf16[64,768]{1,0:T(8,128)(2,1)} %refs_0_.3), channel_id=1, source_target_pairs={{0,4},{1,5},{2,6},{3,7},{4,0},{5,1},{6,2},{7,3},{8,12},{9,13},{10,... | collective-permute-start | bytes 294920 | tf_op jit(solution)/shard_map/ppermute | solution.py:108
  7.2 5.8 %collective-permute-start.3 = (bf16[64,768]{1,0:T(8,128)(2,1)}, bf16[64,768]{1,0:T(8,128)(2,1)S(1)}, u32[]{:S(2)}, u32[]{:S(2)}) collective-permute-start(bf16[64,768]{1,0:T(8,128)(2,1)} %refs_0_.3), channel_id=1, source_target_pairs={{0,6},{1,7},{2,4},{3,5},{4,2},{5,3},{6,0},{7,1},{8,14},{9,15},{10,... | collective-permute-start | bytes 294920 | tf_op jit(solution)/shard_map/ppermute | solution.py:108
  7.6 5.4 %collective-permute-start.7 = (bf16[64,768]{1,0:T(8,128)(2,1)}, bf16[64,768]{1,0:T(8,128)(2,1)S(1)}, u32[]{:S(2)}, u32[]{:S(2)}) collective-permute-start(bf16[64,768]{1,0:T(8,128)(2,1)} %refs_0_.3), channel_id=1, source_target_pairs={{0,1},{1,0},{2,3},{3,2},{4,5},{5,4},{6,7},{7,6},{8,9},{9,8},{10,11... | collective-permute-start | bytes 294920 | tf_op jit(solution)/shard_map/ppermute | solution.py:108
  7.6 11.7 %slice-start.3 = ((s8[9437184]{0:T(1024)(128)(4,1)}), s8[4194304]{0:T(1024)(128)(4,1)S(1)}, s32[]{:S(2)}) async-start(s8[9437184]{0:T(1024)(128)(4,1)} %bitcast.40), calls=%async_computation.5 | async-start | bytes 8388608
  7.6 0.8 %copy-start.5 = (s32[4]{0:T(128)S(1)}, s32[4]{0:T(128)}, u32[]{:S(2)}) copy-start(s32[4]{0:T(128)} %lengths_ref.1) | copy-start | bytes 52
  7.6 0.9 %copy-start.6 = (s32[4,4,4]{2,1,0:T(4,128)S(1)}, s32[4,4,4]{2,1,0:T(4,128)}, u32[]{:S(2)}) copy-start(s32[4,4,4]{2,1,0:T(4,128)} %param.19) | copy-start | bytes 772
  7.6 0.9 %copy-start.7 = (s32[4,4,4]{2,1,0:T(4,128)S(1)}, s32[4,4,4]{2,1,0:T(4,128)}, u32[]{:S(2)}) copy-start(s32[4,4,4]{2,1,0:T(4,128)} %param.18) | copy-start | bytes 772
  7.6 10.5 %copy-start.3 = (bf16[64,768]{1,0:T(8,128)(2,1)S(1)}, bf16[64,768]{1,0:T(8,128)(2,1)}, u32[]{:S(2)}) copy-start(bf16[64,768]{1,0:T(8,128)(2,1)} %refs_0_.3) | copy-start | bytes 294916
  7.6 11.7 %slice-start.4 = ((s8[9437184]{0:T(1024)(128)(4,1)}), s8[4194304]{0:T(1024)(128)(4,1)S(1)}, s32[]{:S(2)}) async-start(s8[9437184]{0:T(1024)(128)(4,1)} %bitcast.40), calls=%async_computation.6 | async-start | bytes 8388608
  7.6 11.7 %slice-start.5 = ((s8[9437184]{0:T(1024)(128)(4,1)}), s8[1048576]{0:T(1024)(128)(4,1)S(1)}, s32[]{:S(2)}) async-start(s8[9437184]{0:T(1024)(128)(4,1)} %bitcast.40), calls=%async_computation.7 | async-start | bytes 2097152
  7.6 11.7 %copy-start.2 = (bf16[12288,64]{0,1:T(8,128)(2,1)S(1)}, bf16[12288,64]{0,1:T(8,128)(2,1)}, u32[]{:S(2)}) copy-start(bf16[12288,64]{0,1:T(8,128)(2,1)} %param.13) | copy-start | bytes 4718596
  7.6 11.7 %copy-start.4 = (f32[12288]{0:T(1024)S(1)}, f32[12288]{0:T(1024)}, u32[]{:S(2)}) copy-start(f32[12288]{0:T(1024)} %param.11) | copy-start | bytes 147460
  9.3 5.7 %collective-permute-start.4 = (bf16[64,768]{1,0:T(8,128)(2,1)S(1)}, bf16[64,768]{1,0:T(8,128)(2,1)S(1)}, u32[]{:S(2)}, u32[]{:S(2)}) collective-permute-start(bf16[64,768]{1,0:T(8,128)(2,1)S(1)} %collective-permute-done.refs_1_), channel_id=1, source_target_pairs={{0,2},{1,3},{2,0},{3,1},{4,6},{5,7},{6,4},{7,5},{8,10},{9,11},{10,... | collective-permute-start | bytes 294920 | tf_op jit(solution)/shard_map/ppermute | solution.py:108
  10.7 5.5 %collective-permute-start.5 = (bf16[64,768]{1,0:T(8,128)(2,1)S(1)}, bf16[64,768]{1,0:T(8,128)(2,1)S(1)}, u32[]{:S(2)}, u32[]{:S(2)}) collective-permute-start(bf16[64,768]{1,0:T(8,128)(2,1)S(1)} %collective-permute-done.refs_1_), channel_id=1, source_target_pairs={{0,4},{1,5},{2,6},{3,7},{4,0},{5,1},{6,2},{7,3},{8,12},{9,13},{10,... | collective-permute-start | bytes 294920 | tf_op jit(solution)/shard_map/ppermute | solution.py:108
  11.7 5.8 %collective-permute-start.6 = (bf16[64,768]{1,0:T(8,128)(2,1)S(1)}, bf16[64,768]{1,0:T(8,128)(2,1)S(1)}, u32[]{:S(2)}, u32[]{:S(2)}) collective-permute-start(bf16[64,768]{1,0:T(8,128)(2,1)S(1)} %collective-permute-done.refs_1_), channel_id=1, source_target_pairs={{0,6},{1,7},{2,4},{3,5},{4,2},{5,3},{6,0},{7,1},{8,14},{9,15},{10,... | collective-permute-start | bytes 294920 | tf_op jit(solution)/shard_map/ppermute | solution.py:108
  13.0 4.5 %collective-permute-start.9 = (bf16[64,768]{1,0:T(8,128)(2,1)S(1)}, bf16[64,768]{1,0:T(8,128)(2,1)S(1)}, u32[]{:S(2)}, u32[]{:S(2)}) collective-permute-start(bf16[64,768]{1,0:T(8,128)(2,1)S(1)} %collective-permute-done.1.refs_2_), channel_id=1, source_target_pairs={{0,1},{1,0},{2,3},{3,2},{4,5},{5,4},{6,7},{7,6},{8,9},{9,8},{10,11... | collective-permute-start | bytes 294920 | tf_op jit(solution)/shard_map/ppermute | solution.py:108
  13.0 5.0 %collective-permute-start.10 = (bf16[64,768]{1,0:T(8,128)(2,1)S(1)}, bf16[64,768]{1,0:T(8,128)(2,1)S(1)}, u32[]{:S(2)}, u32[]{:S(2)}) collective-permute-start(bf16[64,768]{1,0:T(8,128)(2,1)S(1)} %collective-permute-done.2.refs_3_), channel_id=1, source_target_pairs={{0,1},{1,0},{2,3},{3,2},{4,5},{5,4},{6,7},{7,6},{8,9},{9,8},{10,11... | collective-permute-start | bytes 294920 | tf_op jit(solution)/shard_map/ppermute | solution.py:108
  15.0 4.3 %collective-permute-start.8 = (bf16[64,768]{1,0:T(8,128)(2,1)S(1)}, bf16[64,768]{1,0:T(8,128)(2,1)S(1)}, u32[]{:S(2)}, u32[]{:S(2)}) collective-permute-start(bf16[64,768]{1,0:T(8,128)(2,1)S(1)} %collective-permute-done.refs_1_), channel_id=1, source_target_pairs={{0,1},{1,0},{2,3},{3,2},{4,5},{5,4},{6,7},{7,6},{8,9},{9,8},{10,11... | collective-permute-start | bytes 294920 | tf_op jit(solution)/shard_map/ppermute | solution.py:108
  16.2 1.9 %collective-permute-start.11 = (bf16[64,768]{1,0:T(8,128)(2,1)S(1)}, bf16[64,768]{1,0:T(8,128)(2,1)S(1)}, u32[]{:S(2)}, u32[]{:S(2)}) collective-permute-start(bf16[64,768]{1,0:T(8,128)(2,1)S(1)} %collective-permute-done.3.refs_4_), channel_id=1, source_target_pairs={{0,1},{1,0},{2,3},{3,2},{4,5},{5,4},{6,7},{7,6},{8,9},{9,8},{10,11... | collective-permute-start | bytes 294920 | tf_op jit(solution)/shard_map/ppermute | solution.py:108
  17.5 1.8 %collective-permute-start.12 = (bf16[64,768]{1,0:T(8,128)(2,1)S(1)}, bf16[64,768]{1,0:T(8,128)(2,1)S(1)}, u32[]{:S(2)}, u32[]{:S(2)}) collective-permute-start(bf16[64,768]{1,0:T(8,128)(2,1)S(1)} %collective-permute-done.4.refs_5_), channel_id=1, source_target_pairs={{0,1},{1,0},{2,3},{3,2},{4,5},{5,4},{6,7},{7,6},{8,9},{9,8},{10,11... | collective-permute-start | bytes 294920 | tf_op jit(solution)/shard_map/ppermute | solution.py:108
  17.5 1.8 %collective-permute-start.13 = (bf16[64,768]{1,0:T(8,128)(2,1)S(1)}, bf16[64,768]{1,0:T(8,128)(2,1)S(1)}, u32[]{:S(2)}, u32[]{:S(2)}) collective-permute-start(bf16[64,768]{1,0:T(8,128)(2,1)S(1)} %collective-permute-done.5.refs_6_), channel_id=1, source_target_pairs={{0,1},{1,0},{2,3},{3,2},{4,5},{5,4},{6,7},{7,6},{8,9},{9,8},{10,11... | collective-permute-start | bytes 294920 | tf_op jit(solution)/shard_map/ppermute | solution.py:108
  18.0 1.3 %collective-permute-start.14 = (bf16[64,768]{1,0:T(8,128)(2,1)S(1)}, bf16[64,768]{1,0:T(8,128)(2,1)S(1)}, u32[]{:S(2)}, u32[]{:S(2)}) collective-permute-start(bf16[64,768]{1,0:T(8,128)(2,1)S(1)} %collective-permute-done.6.refs_7_), channel_id=1, source_target_pairs={{0,1},{1,0},{2,3},{3,2},{4,5},{5,4},{6,7},{7,6},{8,9},{9,8},{10,11... | collective-permute-start | bytes 294920 | tf_op jit(solution)/shard_map/ppermute | solution.py:108
  18.1 27.3 %slice-start = ((s8[9437184]{0:T(1024)(128)(4,1)}), s8[4194304]{0:T(1024)(128)(4,1)S(1)}, s32[]{:S(2)}) async-start(s8[9437184]{0:T(1024)(128)(4,1)} %bitcast.38), calls=%async_computation.2 | async-start | bytes 8388608
  19.4 14.8 %copy-start = (bf16[4,512,512]{2,1,0:T(8,128)(2,1)S(1)}, bf16[4,512,512]{2,1,0:T(8,128)(2,1)}, u32[]{:S(2)}) copy-start(bf16[4,512,512]{2,1,0:T(8,128)(2,1)} %keys_ref.1) | copy-start | bytes 6291460
  19.4 14.8 %copy-start.1 = (bf16[4,512,512]{2,1,0:T(8,128)(2,1)S(1)}, bf16[4,512,512]{2,1,0:T(8,128)(2,1)}, u32[]{:S(2)}) copy-start(bf16[4,512,512]{2,1,0:T(8,128)(2,1)} %values_ref.1) | copy-start | bytes 6291460
  19.4 26.0 %slice-start.1 = ((s8[9437184]{0:T(1024)(128)(4,1)}), s8[4194304]{0:T(1024)(128)(4,1)S(1)}, s32[]{:S(2)}) async-start(s8[9437184]{0:T(1024)(128)(4,1)} %bitcast.38), calls=%async_computation.3 | async-start | bytes 8388608
  19.4 26.0 %slice-start.2 = ((s8[9437184]{0:T(1024)(128)(4,1)}), s8[1048576]{0:T(1024)(128)(4,1)S(1)}, s32[]{:S(2)}) async-start(s8[9437184]{0:T(1024)(128)(4,1)} %bitcast.38), calls=%async_computation.4 | async-start | bytes 2097152
  46.0 2.4 %collective-permute-start.19 = (bf16[4,64,768]{2,1,0:T(8,128)(2,1)S(1)}, bf16[4,64,768]{2,1,0:T(8,128)(2,1)S(1)}, u32[]{:S(2)}, u32[]{:S(2)}) collective-permute-start(bf16[4,64,768]{2,1,0:T(8,128)(2,1)S(1)} %expand.7), channel_id=1, source_target_pairs={{0,1},{1,0},{2,3},{3,2},{4,5},{5,4},{6,7},{7,6},{8,9},{9,8},{10,11... | collective-permute-start | bytes 1179656 | tf_op jit(solution)/shard_map/ppermute | solution.py:108
  46.7 5.4 %collective-permute-start.15 = (bf16[4,64,768]{2,1,0:T(8,128)(2,1)S(1)}, bf16[4,64,768]{2,1,0:T(8,128)(2,1)S(1)}, u32[]{:S(2)}, u32[]{:S(2)}) collective-permute-start(bf16[4,64,768]{2,1,0:T(8,128)(2,1)S(1)} %expand.5), channel_id=1, source_target_pairs={{0,1},{1,0},{2,3},{3,2},{4,5},{5,4},{6,7},{7,6},{8,9},{9,8},{10,11... | collective-permute-start | bytes 1179656 | tf_op jit(solution)/shard_map/ppermute | solution.py:108
  48.5 4.8 %collective-permute-start.22 = (bf16[64,768]{1,0:T(8,128)(2,1)S(1)}, bf16[64,768]{1,0:T(8,128)(2,1)S(1)}, u32[]{:S(2)}, u32[]{:S(2)}) collective-permute-start(bf16[64,768]{1,0:T(8,128)(2,1)S(1)} %get-tuple-element.23), channel_id=1, source_target_pairs={{0,2},{1,3},{2,0},{3,1},{4,6},{5,7},{6,4},{7,5},{8,10},{9,11},{10,... | collective-permute-start | bytes 294920 | tf_op jit(solution)/shard_map/ppermute | solution.py:108
  48.8 6.9 %collective-permute-start.21 = (bf16[64,768]{1,0:T(8,128)(2,1)S(1)}, bf16[64,768]{1,0:T(8,128)(2,1)S(1)}, u32[]{:S(2)}, u32[]{:S(2)}) collective-permute-start(bf16[64,768]{1,0:T(8,128)(2,1)S(1)} %get-tuple-element.24), channel_id=1, source_target_pairs={{0,4},{1,5},{2,6},{3,7},{4,0},{5,1},{6,2},{7,3},{8,12},{9,13},{10,... | collective-permute-start | bytes 294920 | tf_op jit(solution)/shard_map/ppermute | solution.py:108
  49.4 8.5 %collective-permute-start.20 = (bf16[64,768]{1,0:T(8,128)(2,1)S(1)}, bf16[64,768]{1,0:T(8,128)(2,1)S(1)}, u32[]{:S(2)}, u32[]{:S(2)}) collective-permute-start(bf16[64,768]{1,0:T(8,128)(2,1)S(1)} %get-tuple-element.22), channel_id=1, source_target_pairs={{0,6},{1,7},{2,4},{3,5},{4,2},{5,3},{6,0},{7,1},{8,14},{9,15},{10,... | collective-permute-start | bytes 294920 | tf_op jit(solution)/shard_map/ppermute | solution.py:108
  52.1 6.2 %collective-permute-start.18 = (bf16[64,768]{1,0:T(8,128)(2,1)S(1)}, bf16[64,768]{1,0:T(8,128)(2,1)S(1)}, u32[]{:S(2)}, u32[]{:S(2)}) collective-permute-start(bf16[64,768]{1,0:T(8,128)(2,1)S(1)} %get-tuple-element.20), channel_id=1, source_target_pairs={{0,2},{1,3},{2,0},{3,1},{4,6},{5,7},{6,4},{7,5},{8,10},{9,11},{10,... | collective-permute-start | bytes 294920 | tf_op jit(solution)/shard_map/ppermute | solution.py:108
  52.4 6.2 %collective-permute-start.17 = (bf16[64,768]{1,0:T(8,128)(2,1)S(1)}, bf16[64,768]{1,0:T(8,128)(2,1)S(1)}, u32[]{:S(2)}, u32[]{:S(2)}) collective-permute-start(bf16[64,768]{1,0:T(8,128)(2,1)S(1)} %get-tuple-element.21), channel_id=1, source_target_pairs={{0,4},{1,5},{2,6},{3,7},{4,0},{5,1},{6,2},{7,3},{8,12},{9,13},{10,... | collective-permute-start | bytes 294920 | tf_op jit(solution)/shard_map/ppermute | solution.py:108
  53.3 8.6 %collective-permute-start.16 = (bf16[64,768]{1,0:T(8,128)(2,1)S(1)}, bf16[64,768]{1,0:T(8,128)(2,1)S(1)}, u32[]{:S(2)}, u32[]{:S(2)}) collective-permute-start(bf16[64,768]{1,0:T(8,128)(2,1)S(1)} %get-tuple-element.19), channel_id=1, source_target_pairs={{0,6},{1,7},{2,4},{3,5},{4,2},{5,3},{6,0},{7,1},{8,14},{9,15},{10,... | collective-permute-start | bytes 294920 | tf_op jit(solution)/shard_map/ppermute | solution.py:108
  57.9 6.1 %collective-permute-start.23 = (bf16[64,768]{1,0:T(8,128)(2,1)S(1)}, bf16[64,768]{1,0:T(8,128)(2,1)S(1)}, u32[]{:S(2)}, u32[]{:S(2)}) collective-permute-start(bf16[64,768]{1,0:T(8,128)(2,1)S(1)} %fusion.7), channel_id=1, source_target_pairs={{0,8},{1,9},{2,10},{3,11},{4,12},{5,13},{6,14},{7,15},{8,0},{9,1},... | collective-permute-start | bytes 294920 | tf_op jit(solution)/shard_map/ppermute | solution.py:108
